TPU v7x, 32 devices: a whole 2x2x4 slice. The times are simulated.
32 devices in a mesh: groups: 1, rows: 32 (over z, y, x, core).
Axes of the slice: x: 2, y: 2, z: 4, core: 2. Of those that a mesh axis runs over, the one named last changes fastest.
Arguments:
- tokens: bfloat16 [384, 8192], P(('groups', 'rows')), may hold values from -6 to 6
- gate_weight: bfloat16 [8192, 14336], P('rows'), may hold values from -0.0625 to 0.0625
- up_weight: bfloat16 [8192, 14336], P('rows'), may hold values from -0.0625 to 0.0625
- skew_params: float32 [2, 2, 128, 64, 64], P(None, None, 'rows'), may hold values from -0.3125 to 0.3125
- section_bits: int32 [2, 13], replicated, may hold values from 0 to 12, each once within a row
- upstream: bfloat16 [384, 14336], P('groups', 'rows'), may hold values from -0.3125 to 0.3125
Outputs:
- activation: bfloat16 [384, 14336], P('groups', 'rows')
- skew_grad: float32 [2, 2, 128, 64, 64], P('groups', None, 'rows')
Inputs may be any that keep to these rules, and one draw needn't show every extreme that they name: Each row of section_bits names every one of the 13 bit positions once.
All inputs are finite; a program needn't handle non-finite values.
Results may differ from a plain program's by a relative error of at most 0.0093.
Values may be sent and summed in bfloat16 or wider, within the bound.
A program may use at most 192 MiB of HBM per device.

v0:
```python
import jax
import jax.numpy as jnp
from jax import lax
from jax.sharding import PartitionSpec as P


def cayley(skew_blocks):
    extent = skew_blocks.shape[-1]
    identity = jnp.eye(extent, dtype=jnp.float32)
    generator = skew_blocks - jnp.swapaxes(skew_blocks, -1, -2)
    minus_part = identity - generator
    squared = jnp.einsum(
        "...ij,...jk->...ik", minus_part, minus_part, precision=lax.Precision.HIGHEST
    )
    normal = identity - jnp.einsum(
        "...ij,...jk->...ik", generator, generator, precision=lax.Precision.HIGHEST
    )
    lower_factor = jnp.linalg.cholesky(normal)
    halfway = lax.linalg.triangular_solve(lower_factor, squared, left_side=True, lower=True)
    return lax.linalg.triangular_solve(
        lower_factor, halfway, left_side=True, lower=True, transpose_a=True
    )


def slot_order(section_row, extent):
    positions = jnp.arange(extent, dtype=jnp.int32)
    places = jnp.arange(section_row.shape[0], dtype=jnp.int32)
    digits = jnp.right_shift(positions[:, None], places[None, :]) & 1
    return jnp.sum(jnp.left_shift(digits, section_row[None, :]), axis=1)


def inverse_order(section_row, extent):
    positions = jnp.arange(extent, dtype=jnp.int32)
    places = jnp.arange(section_row.shape[0], dtype=jnp.int32)
    digits = jnp.right_shift(positions[:, None], section_row[None, :]) & 1
    return jnp.sum(jnp.left_shift(digits, places[None, :]), axis=1)


def rotate_columns(columns, rotation, orders, inverses):
    kept_inputs = []
    current = columns
    index = orders[0]
    block_count = rotation.shape[1]
    col_count = columns.shape[1]
    section_total = len(orders)
    for section_at in range(section_total):
        permuted = current[index]
        mixed_rows = jnp.einsum(
            "kji,kic->kjc",
            rotation[section_at],
            permuted.reshape(block_count, -1, col_count),
            preferred_element_type=jnp.float32,
        ).astype(jnp.bfloat16)
        kept_inputs.append(permuted)
        current = mixed_rows.reshape(columns.shape)
        if section_at + 1 < section_total:
            index = inverses[section_at][orders[section_at + 1]]
        else:
            index = inverses[section_at]
    return (current[index], kept_inputs)


def unrotate(grad_top, rotation, orders, inverses):
    block_count = rotation.shape[1]
    col_count = grad_top.shape[1]
    section_total = len(orders)
    slot_grads = [None] * section_total
    current = grad_top
    index = orders[section_total - 1]
    for section_at in reversed(range(section_total)):
        permuted = current[index]
        slot_grads[section_at] = permuted
        if section_at > 0:
            pulled = jnp.einsum(
                "kji,kjc->kic",
                rotation[section_at],
                permuted.reshape(block_count, -1, col_count),
                preferred_element_type=jnp.float32,
            ).astype(jnp.bfloat16)
            current = pulled.reshape(grad_top.shape)
            index = inverses[section_at][orders[section_at - 1]]
    return slot_grads


def block_products(slot_grad, slot_input, block_count):
    col_count = slot_grad.shape[-1]
    return jnp.einsum(
        "kjc,kic->kji",
        slot_grad.reshape(block_count, -1, col_count),
        slot_input.reshape(block_count, -1, col_count),
        preferred_element_type=jnp.float32,
    )


def shards(tokens, gate_weight, up_weight, skew_params, section_bits, upstream):
    extent = skew_params.shape[-1]
    model_width = tokens.shape[1]
    block_count = model_width // extent
    section_count = section_bits.shape[0]
    own_rotation, pullback = jax.vjp(cayley, skew_params)
    rotation = lax.all_gather(own_rotation.astype(jnp.bfloat16), "rows", axis=2, tiled=True)
    orders = [
        slot_order(section_bits[section_at], model_width) for section_at in range(section_count)
    ]
    inverses = [
        inverse_order(section_bits[section_at], model_width) for section_at in range(section_count)
    ]
    all_tokens = lax.all_gather(tokens, "rows", axis=0, tiled=True)
    gate_cols, up_cols = (
        lax.all_to_all(gate_weight, "rows", split_axis=1, concat_axis=0, tiled=True),
        lax.all_to_all(up_weight, "rows", split_axis=1, concat_axis=0, tiled=True),
    )
    rotated_gate, gate_inputs = rotate_columns(gate_cols, rotation[0], orders, inverses)
    rotated_up, up_inputs = rotate_columns(up_cols, rotation[1], orders, inverses)
    gate_pre = jnp.dot(all_tokens, rotated_gate, preferred_element_type=jnp.float32)
    up_pre = jnp.dot(all_tokens, rotated_up, preferred_element_type=jnp.float32)
    sigmoid_val = jax.nn.sigmoid(gate_pre)
    silu_val = gate_pre * sigmoid_val
    activation = (silu_val * up_pre).astype(jnp.bfloat16)
    cotangent = upstream.astype(jnp.float32)
    gate_grad = (cotangent * up_pre * sigmoid_val * (1.0 + gate_pre * (1.0 - sigmoid_val))).astype(
        jnp.bfloat16
    )
    up_grad = (cotangent * silu_val).astype(jnp.bfloat16)
    contract = (((0,), (0,)), ((), ()))
    gate_top = lax.dot_general(
        all_tokens, gate_grad, contract, preferred_element_type=jnp.float32
    ).astype(jnp.bfloat16)
    up_top = lax.dot_general(
        all_tokens, up_grad, contract, preferred_element_type=jnp.float32
    ).astype(jnp.bfloat16)
    gate_slots = unrotate(gate_top, rotation[0], orders, inverses)
    up_slots = unrotate(up_top, rotation[1], orders, inverses)
    gate_terms = jnp.stack(
        [
            block_products(gate_slots[section_at], gate_inputs[section_at], block_count)
            for section_at in range(section_count)
        ]
    )
    up_terms = jnp.stack(
        [
            block_products(up_slots[section_at], up_inputs[section_at], block_count)
            for section_at in range(section_count)
        ]
    )
    own_sums = lax.psum_scatter(
        jnp.stack((gate_terms, up_terms)), "rows", scatter_dimension=2, tiled=True
    )
    skew_grad = pullback(own_sums)[0]
    return (activation, skew_grad)


def solution(mesh):
    placed = (
        P(("groups", "rows"), None),
        P("rows", None),
        P("rows", None),
        P(None, None, "rows", None, None),
        P(),
        P("groups", "rows"),
    )
    return jax.shard_map(
        shards,
        mesh=mesh,
        in_specs=placed,
        out_specs=(P("groups", "rows"), P("groups", None, "rows", None, None)),
        check_vma=False,
    )
```

profile of v0, /device:TPU:0, one launch (start us, length us, event | category | flops | bytes accessed | tf_op | source)
XLA Modules:
  0.0 1387.2 jit_solution(2663491135916769819)
XLA Ops:
  7.2 10.2 copy.86
  25.5 10.2 copy.88
  35.7 190.3 %all-to-all-done = bf16[256,32,448]{0,2,1:T(8,128)(2,1)} async-done(((bf16[256,32,448]{0,2,1:T(8,128)(2,1)}), bf16[256,32,448]{0,2,1:T(8,128)(2,1)}, u32[]{:S(2)}, u32[]{:S(2)}) %all-to-all-start) | async-done | bytes 7340064 | tf_op jit(solution)/shard_map/all_to_all | solution.py:110
  231.0 93.8 %custom-call.14 = f32[2,2,4,64,64]{4,3,2,1,0:T(8,128)S(1)} custom-call(f32[2,2,4,64,64]{4,3,2,1,0:T(8,128)S(1)} %fusion.35), custom_call_target="Cholesky" | custom-call | tf_op jit(solution)/shard_map/jvp(jit(cholesky))/cholesky | solution.py:18
  326.7 78.6 %custom-call.22 = f32[2,2,4,1,64,64]{4,5,3,2,1,0:T(8,128)S(1)} custom-call(f32[2,2,4,1,64,64]{5,4,3,2,1,0:T(8,128)S(1)} %get-tuple-element.9), custom_call_target="InvertDiagBlocksLowerTriangular" | custom-call | tf_op jit(solution)/shard_map/jvp()/triangular_solve/custom-call.0 | solution.py:20
  410.2 46.0 %gather_fusion.1 = s32[8192]{0:T(1024)S(1)} fusion(s32[8192]{0:T(1024)S(1)} %get-tuple-element.19, s32[8192]{0:T(1024)S(1)} %broadcast_clamp_fusion.3), kind=kCustom, calls=%fused_computation.1 | custom fusion | bytes 98304 | tf_op jit(solution)/shard_map/gather | solution.py:57
  456.3 45.5 %gather_fusion.8 = s32[8192]{0:T(1024)S(1)} fusion(s32[8192]{0:T(1024)S(1)} %get-tuple-element.4, s32[8192]{0:T(1024)S(1)} %broadcast_clamp_fusion.4), kind=kCustom, calls=%fused_computation.8 | custom fusion | bytes 98304 | tf_op jit(solution)/shard_map/gather | solution.py:81
  511.4 11.0 copy.87
  522.4 38.4 %gather_fusion = bf16[8192,448]{1,0:T(8,128)(2,1)} fusion(bf16[8192,448]{1,0:T(8,128)(2,1)} %bitcast.194, s32[8192]{0:T(1024)S(1)} %broadcast_clamp_fusion.4), kind=kCustom, calls=%fused_computation | custom fusion | bytes 14712832 | tf_op jit(solution)/shard_map/gather | solution.py:47
  560.8 11.0 copy.89
  571.8 38.4 %gather_fusion.4 = bf16[8192,448]{1,0:T(8,128)(2,1)} fusion(bf16[8192,448]{1,0:T(8,128)(2,1)} %bitcast.193, s32[8192]{0:T(1024)S(1)} %broadcast_clamp_fusion.4), kind=kCustom, calls=%fused_computation.4 | custom fusion | bytes 14712832 | tf_op jit(solution)/shard_map/gather | solution.py:47
  619.8 38.4 %gather_fusion.2 = bf16[8192,448]{1,0:T(8,128)(2,1)} fusion(bf16[8192,448]{1,0:T(8,128)(2,1)} %bitcast.191, s32[8192]{0:T(1024)S(1)} %broadcast_clamp_fusion.2), kind=kCustom, calls=%fused_computation.2 | custom fusion | bytes 14712832 | tf_op jit(solution)/shard_map/gather | solution.py:47
  667.7 38.6 %gather_fusion.5 = bf16[8192,448]{1,0:T(8,128)(2,1)} fusion(bf16[8192,448]{1,0:T(8,128)(2,1)} %bitcast.188, s32[8192]{0:T(1024)S(1)} %broadcast_clamp_fusion.2), kind=kCustom, calls=%fused_computation.5 | custom fusion | bytes 14712832 | tf_op jit(solution)/shard_map/gather | solution.py:47
  715.9 38.4 %gather_fusion.3 = bf16[8192,448]{1,0:T(8,128)(2,1)} fusion(bf16[8192,448]{1,0:T(8,128)(2,1)} %bitcast.192, s32[8192]{0:T(1024)S(1)} %broadcast_clamp_fusion.1), kind=kCustom, calls=%fused_computation.3 | custom fusion | bytes 14712832 | tf_op jit(solution)/shard_map/gather | solution.py:60
  763.8 38.4 %gather_fusion.6 = bf16[8192,448]{1,0:T(8,128)(2,1)} fusion(bf16[8192,448]{1,0:T(8,128)(2,1)} %bitcast.189, s32[8192]{0:T(1024)S(1)} %broadcast_clamp_fusion.1), kind=kCustom, calls=%fused_computation.6 | custom fusion | bytes 14712832 | tf_op jit(solution)/shard_map/gather | solution.py:60
  825.8 11.0 copy.94
  836.9 38.7 %gather_fusion.10 = bf16[8192,448]{1,0:T(8,128)(2,1)} fusion(bf16[8192,448]{1,0:T(8,128)(2,1)} %copy.94, s32[8192]{0:T(1024)S(1)} %copy-done.15), kind=kCustom, calls=%fused_computation.10 | custom fusion | bytes 14712832 | tf_op jit(solution)/shard_map/gather | solution.py:71
  895.4 38.4 %gather_fusion.11 = bf16[8192,448]{1,0:T(8,128)(2,1)} fusion(bf16[8192,448]{1,0:T(8,128)(2,1)} %bitcast.190, s32[8192]{0:T(1024)S(1)} %copy-done.16), kind=kCustom, calls=%fused_computation.11 | custom fusion | bytes 14712832 | tf_op jit(solution)/shard_map/gather | solution.py:71
  952.7 11.0 copy.92
  963.7 38.5 %gather_fusion.7 = bf16[8192,448]{1,0:T(8,128)(2,1)} fusion(bf16[8192,448]{1,0:T(8,128)(2,1)} %copy.92, s32[8192]{0:T(1024)S(1)} %copy-done.15), kind=kCustom, calls=%fused_computation.7 | custom fusion | bytes 14712832 | tf_op jit(solution)/shard_map/gather | solution.py:71
  1002.3 10.2 convolution_bitcast_fusion.2
  1022.1 38.4 %gather_fusion.9 = bf16[8192,448]{1,0:T(8,128)(2,1)} fusion(bf16[8192,448]{1,0:T(8,128)(2,1)} %bitcast.187, s32[8192]{0:T(1024)S(1)} %copy-done.16), kind=kCustom, calls=%fused_computation.9 | custom fusion | bytes 14712832 | tf_op jit(solution)/shard_map/gather | solution.py:71
  1085.1 79.7 %custom-call.26 = f32[2,2,4,1,64,64]{4,5,3,2,1,0:T(8,128)S(1)} custom-call(f32[2,2,4,1,64,64]{5,4,3,2,1,0:T(8,128)} %get-tuple-element.8), custom_call_target="InvertDiagBlocksLowerTriangular" | custom-call | tf_op jit(solution)/shard_map/transpose(jvp(jit(cholesky)))/triangular_solve/custom-call.0 | solution.py:18
  1164.9 199.9 %all-reduce.3.cloned.1.call-done = f32[2,2,128,64,64]{4,3,2,1,0:T(8,128)} async-done(((f32[2,2,128,64,64]{4,3,2,1,0:T(8,128)}), f32[2,2,128,64,64]{4,3,2,1,0:T(8,128)}) %all-reduce.3.cloned.1.call-update) | async-done | bytes 8388624
  (128 shorter events, 179.6 us)
Async XLA Ops:
  17.4 208.6 %all-to-all-start = ((bf16[256,32,448]{0,2,1:T(8,128)(2,1)}), bf16[256,32,448]{0,2,1:T(8,128)(2,1)}, u32[]{:S(2)}, u32[]{:S(2)}) async-start(bf16[256,32,448]{0,2,1:T(8,128)(2,1)} %bitcast.210), calls=%async_computation | async-start | bytes 14680064 | tf_op jit(solution)/shard_map/all_to_all | solution.py:110
  24.8 477.9 %all-gather.6.cloned.1.call-start = ((), (), s32[]{:S(2)}) async-start(), calls=%async_computation.3 | async-start | bytes 8650752 | tf_op jit(solution)/shard_map/all_gather | solution.py:108
  35.7 194.0 %copy-start.8 = (f32[2,2,4,64,64]{4,3,2,1,0:T(8,128)S(1)}, f32[2,2,4,64,64]{4,3,2,1,0:T(8,128)}, u32[]{:S(2)}) copy-start(f32[2,2,4,64,64]{4,3,2,1,0:T(8,128)} %param.13) | copy-start | bytes 786436
  226.0 334.8 %all-to-all-start.1 = ((bf16[256,32,448]{0,2,1:T(8,128)(2,1)}), bf16[256,32,448]{0,2,1:T(8,128)(2,1)}, u32[]{:S(2)}, u32[]{:S(2)}) async-start(bf16[256,32,448]{0,2,1:T(8,128)(2,1)} %bitcast.209), calls=%async_computation.1 | async-start | bytes 14680064 | tf_op jit(solution)/shard_map/all_to_all | solution.py:111
  229.7 179.8 %copy-start.23 = (s32[2,13]{1,0:T(2,128)S(1)}, s32[2,13]{1,0:T(2,128)}, u32[]{:S(2)}) copy-start(s32[2,13]{1,0:T(2,128)} %param.14) | copy-start | bytes 316
  229.7 380.5 %all-gather.4.cloned.1.call-start = ((), (), s32[]{:S(2)}) async-start(), calls=%async_computation.2 | async-start | bytes 8650752 | tf_op jit(solution)/shard_map/all_gather | solution.py:101
  230.0 179.5 %copy-start = (f32[2,2,4,64,64]{4,3,2,1,0:T(8,128)}, f32[2,2,4,64,64]{4,3,2,1,0:T(8,128)S(1)}, u32[]{:S(2)}) copy-start(f32[2,2,4,64,64]{4,3,2,1,0:T(8,128)S(1)} %bitcast_subtract_fusion.1) | copy-start | bytes 786436
  230.9 225.4 %copy-start.12 = (f32[64,64]{1,0:T(8,128)}, f32[64,64]{1,0:T(8,128)S(1)}, u32[]{:S(2)}) copy-start(f32[64,64]{1,0:T(8,128)S(1)} %get-tuple-element.21) | copy-start | bytes 49156
  405.3 50.9 %copy-start.2 = (f32[2,2,4,1,64,64]{4,5,3,2,1,0:T(8,128)}, f32[2,2,4,1,64,64]{4,5,3,2,1,0:T(8,128)S(1)}, u32[]{:S(2)}) copy-start(f32[2,2,4,1,64,64]{4,5,3,2,1,0:T(8,128)S(1)} %custom-call.22) | copy-start | bytes 786436
  409.4 955.3 %all-reduce.3.cloned.1.call-start = ((), (), s32[]{:S(2)}) async-start(), calls=%async_computation.4 | async-start | bytes 33554432
  410.2 46.0 %copy-start.14 = (s32[8192]{0:T(1024)}, s32[8192]{0:T(1024)S(1)}, u32[]{:S(2)}) copy-start(s32[8192]{0:T(1024)S(1)} %broadcast_clamp_fusion.3) | copy-start | bytes 98308
  802.2 9.3 copy-start.5
  802.2 17.5 %slice-start = ((s8[6291456]{0:T(1024)(128)(4,1)}), s8[4194304]{0:T(1024)(128)(4,1)S(1)}, s32[]{:S(2)}) async-start(s8[6291456]{0:T(1024)(128)(4,1)} %bitcast.211), calls=%async_computation.5 | async-start | bytes 8388608
  825.8 11.1 copy-start.15
  885.8 9.7 copy-start.16
  1085.0 279.8 %copy-start.3 = (f32[2,2,4,1,64,64]{4,5,3,2,1,0:T(8,128)S(1)}, f32[2,2,4,1,64,64]{4,5,3,2,1,0:T(8,128)}, u32[]{:S(2)}) copy-start(f32[2,2,4,1,64,64]{4,5,3,2,1,0:T(8,128)} %copy-done.2) | copy-start | bytes 786436
  1085.0 281.8 %copy-start.7 = (f32[2,2,4,64,64]{4,3,2,1,0:T(8,128)S(1)}, f32[2,2,4,64,64]{4,3,2,1,0:T(8,128)}, u32[]{:S(2)}) copy-start(f32[2,2,4,64,64]{4,3,2,1,0:T(8,128)} %copy-done.6) | copy-start | bytes 786436
  1085.0 283.4 %copy-start.9 = (f32[2,2,4,64,64]{4,3,2,1,0:T(8,128)S(1)}, f32[2,2,4,64,64]{4,3,2,1,0:T(8,128)}, u32[]{:S(2)}) copy-start(f32[2,2,4,64,64]{4,3,2,1,0:T(8,128)} %get-tuple-element.15) | copy-start | bytes 786436
  1085.0 285.5 %copy-start.18 = (pred[64,64]{1,0:T(8,128)(4,1)S(1)}, pred[64,64]{1,0:T(8,128)(4,1)}, u32[]{:S(2)}) copy-start(pred[64,64]{1,0:T(8,128)(4,1)} %copy-done.17) | copy-start | bytes 12292
  1085.1 287.2 %copy-start.11 = (f32[2,2,4,64,64]{4,3,2,1,0:T(8,128)S(1)}, f32[2,2,4,64,64]{4,3,2,1,0:T(8,128)}, u32[]{:S(2)}) copy-start(f32[2,2,4,64,64]{4,3,2,1,0:T(8,128)} %copy-done.10) | copy-start | bytes 786436
  1085.1 287.2 %copy-start.22 = (pred[2,2,4]{2,1,0:T(4,128)(4,1)S(1)}, pred[2,2,4]{2,1,0:T(4,128)(4,1)}, u32[]{:S(2)}) copy-start(pred[2,2,4]{2,1,0:T(4,128)(4,1)} %copy-done.21) | copy-start | bytes 52
  1164.9 210.3 %copy-start.1 = (f32[2,2,4,64,64]{4,3,2,1,0:T(8,128)S(1)}, f32[2,2,4,64,64]{4,3,2,1,0:T(8,128)}, u32[]{:S(2)}) copy-start(f32[2,2,4,64,64]{4,3,2,1,0:T(8,128)} %copy-done) | copy-start | bytes 786436
  1164.9 210.3 %copy-start.19 = (pred[64,64]{1,0:T(8,128)(4,1)S(1)}, pred[64,64]{1,0:T(8,128)(4,1)}, u32[]{:S(2)}) copy-start(pred[64,64]{1,0:T(8,128)(4,1)} %get-tuple-element.12) | copy-start | bytes 12292
  1164.9 210.3 %copy-start.20 = (pred[64,64]{1,0:T(8,128)(4,1)S(1)}, pred[64,64]{1,0:T(8,128)(4,1)}, u32[]{:S(2)}) copy-start(pred[64,64]{1,0:T(8,128)(4,1)} %get-tuple-element.13) | copy-start | bytes 12292
  (8 other events, 35.4 us)
Sparse Core Ops, SparseCore 0:
  28.5 163.7 all-gather.5
  409.6 78.5 all-gather.3
  1085.2 279.5 all-reduce.2
where the time goes:
time: 1400 us; the launch traced here: 1390 us
  local copies, waits for them, and re-layouts  551 us (39%)
  waiting for transfers between devices  391 us (28%)
  other arithmetic  271 us (19%)
  matrix products  149 us (11%)
  between operations  14.6 us (1%)
    unnamed x4, waiting for transfers between devices  201 us
    all_to_all x1, waiting for transfers between devices, shards(): lax.all_to_all(gate_weight, 'rows', split_axis=1, concat_axis=0, tiled=True)  190 us
    another operation x6, other arithmetic, cayley(): lower_factor = jnp.linalg.cholesky(normal)  175 us
    gather x4, local copies, waits for them, and re-layouts, unrotate(): permuted = current[index]  154 us
    gather x4, local copies, waits for them, and re-layouts, rotate_columns(): permuted = current[index]  154 us
    another operation x1, other arithmetic, cayley(): lax.linalg.triangular_solve(lower_factor, halfway, left_side=True, lower=...  78.6 us
    gather x2, local copies, waits for them, and re-layouts, rotate_columns(): return (current[index], kept_inputs)  76.7 us
    gather x1, local copies, waits for them, and re-layouts, rotate_columns(): index = inverses[section_at][orders[section_at + 1]]  46 us
  transfers between devices with their start and end apart: 5, of which 2 were waited for; matrix products, arithmetic and copies ran while one was open for 34% of the time, Pallas kernels for 0%

commit v1 on v0

--- a/solution.py
+++ b/solution.py
@@ -107,7 +107,12 @@
     ]
     all_tokens = lax.all_gather(tokens, "rows", axis=0, tiled=True)
     gate_cols, up_cols = (
-        lax.all_to_all(gate_weight, "rows", split_axis=1, concat_axis=0, tiled=True),
+        jnp.concatenate(
+            lax.all_to_all(
+                jnp.stack(jnp.split(gate_weight, lax.axis_size("rows"), axis=1)), "rows", 0, 0
+            ),
+            axis=0,
+        ),
         lax.all_to_all(up_weight, "rows", split_axis=1, concat_axis=0, tiled=True),
     )
     rotated_gate, gate_inputs = rotate_columns(gate_cols, rotation[0], orders, inverses)

time: 1400 us -> 1470 us (1.050)
  local copies, waits for them, and re-layouts: 551 us -> 626 us
    unnamed x58 -> x122, local copies, waits for them, and re-layouts: 30.3 us -> 96.1 us
  transfers between devices with their start and end apart: 5 -> 5, of which waited for: 2 -> 2; matrix products, arithmetic and copies ran while one was open for 34% -> 32% of each run, Pallas kernels for 0% -> 0%
where the time goes in v1:
time: 1470 us; the launch traced here: 1460 us
  local copies, waits for them, and re-layouts  626 us (43%)
  waiting for transfers between devices  391 us (27%)
  other arithmetic  271 us (18%)
  matrix products  149 us (10%)
  between operations  15 us (1%)
    unnamed x4, waiting for transfers between devices  200 us
    all_to_all x1, waiting for transfers between devices, shards(): lax.all_to_all(jnp.stack(jnp.split(gate_weight, lax.axis_size('rows'), ax...  190 us
    another operation x6, other arithmetic, cayley(): lower_factor = jnp.linalg.cholesky(normal)  175 us
    gather x4, local copies, waits for them, and re-layouts, unrotate(): permuted = current[index]  153 us
    gather x4, local copies, waits for them, and re-layouts, rotate_columns(): permuted = current[index]  153 us
    unnamed x122, local copies, waits for them, and re-layouts  96.1 us
    another operation x1, other arithmetic, cayley(): lax.linalg.triangular_solve(lower_factor, halfway, left_side=True, lower=...  78.6 us
    gather x2, local copies, waits for them, and re-layouts, rotate_columns(): return (current[index], kept_inputs)  76.4 us
  transfers between devices with their start and end apart: 5, of which 2 were waited for; matrix products, arithmetic and copies ran while one was open for 32% of the time, Pallas kernels for 0%

profile of v1, /device:TPU:0, one launch (start us, length us, event | category | flops | bytes accessed | tf_op | source)
XLA Modules:
  0.0 1462.4 jit_solution(16187743604003416157)
XLA Ops:
  102.0 10.2 copy.147
  112.2 190.3 %all-to-all-done = bf16[32,256,448]{1,2,0:T(8,128)(2,1)} async-done(((bf16[32,256,448]{1,2,0:T(8,128)(2,1)}), bf16[32,256,448]{1,2,0:T(8,128)(2,1)}, u32[]{:S(2)}, u32[]{:S(2)}) %all-to-all-start) | async-done | bytes 7340064 | tf_op jit(solution)/shard_map/all_to_all | solution.py:111
  308.0 93.8 %custom-call.14 = f32[2,2,4,64,64]{4,3,2,1,0:T(8,128)S(1)} custom-call(f32[2,2,4,64,64]{4,3,2,1,0:T(8,128)S(1)} %fusion.35), custom_call_target="Cholesky" | custom-call | tf_op jit(solution)/shard_map/jvp(jit(cholesky))/cholesky | solution.py:18
  403.7 78.6 %custom-call.22 = f32[2,2,4,1,64,64]{4,5,3,2,1,0:T(8,128)S(1)} custom-call(f32[2,2,4,1,64,64]{5,4,3,2,1,0:T(8,128)S(1)} %get-tuple-element.41), custom_call_target="InvertDiagBlocksLowerTriangular" | custom-call | tf_op jit(solution)/shard_map/jvp()/triangular_solve/custom-call.0 | solution.py:20
  487.2 45.7 %gather_fusion.1 = s32[8192]{0:T(1024)S(1)} fusion(s32[8192]{0:T(1024)S(1)} %get-tuple-element.51, s32[8192]{0:T(1024)S(1)} %broadcast_clamp_fusion.3), kind=kCustom, calls=%fused_computation.1 | custom fusion | bytes 98304 | tf_op jit(solution)/shard_map/gather | solution.py:57
  533.0 45.5 %gather_fusion.8 = s32[8192]{0:T(1024)S(1)} fusion(s32[8192]{0:T(1024)S(1)} %get-tuple-element.4, s32[8192]{0:T(1024)S(1)} %broadcast_clamp_fusion.4), kind=kCustom, calls=%fused_computation.8 | custom fusion | bytes 98304 | tf_op jit(solution)/shard_map/gather | solution.py:81
  588.1 11.0 copy.146
  599.0 38.3 %gather_fusion = bf16[8192,448]{1,0:T(8,128)(2,1)} fusion(bf16[8192,448]{1,0:T(8,128)(2,1)} %bitcast.256, s32[8192]{0:T(1024)S(1)} %broadcast_clamp_fusion.4), kind=kCustom, calls=%fused_computation | custom fusion | bytes 14712832 | tf_op jit(solution)/shard_map/gather | solution.py:47
  637.3 11.0 copy.148
  648.3 38.2 %gather_fusion.4 = bf16[8192,448]{1,0:T(8,128)(2,1)} fusion(bf16[8192,448]{1,0:T(8,128)(2,1)} %bitcast.255, s32[8192]{0:T(1024)S(1)} %broadcast_clamp_fusion.4), kind=kCustom, calls=%fused_computation.4 | custom fusion | bytes 14712832 | tf_op jit(solution)/shard_map/gather | solution.py:47
  696.1 38.2 %gather_fusion.2 = bf16[8192,448]{1,0:T(8,128)(2,1)} fusion(bf16[8192,448]{1,0:T(8,128)(2,1)} %bitcast.253, s32[8192]{0:T(1024)S(1)} %broadcast_clamp_fusion.2), kind=kCustom, calls=%fused_computation.2 | custom fusion | bytes 14712832 | tf_op jit(solution)/shard_map/gather | solution.py:47
  743.9 38.4 %gather_fusion.5 = bf16[8192,448]{1,0:T(8,128)(2,1)} fusion(bf16[8192,448]{1,0:T(8,128)(2,1)} %bitcast.250, s32[8192]{0:T(1024)S(1)} %broadcast_clamp_fusion.2), kind=kCustom, calls=%fused_computation.5 | custom fusion | bytes 14712832 | tf_op jit(solution)/shard_map/gather | solution.py:47
  792.0 38.2 %gather_fusion.3 = bf16[8192,448]{1,0:T(8,128)(2,1)} fusion(bf16[8192,448]{1,0:T(8,128)(2,1)} %bitcast.254, s32[8192]{0:T(1024)S(1)} %broadcast_clamp_fusion.1), kind=kCustom, calls=%fused_computation.3 | custom fusion | bytes 14712832 | tf_op jit(solution)/shard_map/gather | solution.py:60
  839.8 38.2 %gather_fusion.6 = bf16[8192,448]{1,0:T(8,128)(2,1)} fusion(bf16[8192,448]{1,0:T(8,128)(2,1)} %bitcast.251, s32[8192]{0:T(1024)S(1)} %broadcast_clamp_fusion.1), kind=kCustom, calls=%fused_computation.6 | custom fusion | bytes 14712832 | tf_op jit(solution)/shard_map/gather | solution.py:60
  901.7 11.1 copy.153
  912.8 38.4 %gather_fusion.10 = bf16[8192,448]{1,0:T(8,128)(2,1)} fusion(bf16[8192,448]{1,0:T(8,128)(2,1)} %copy.153, s32[8192]{0:T(1024)S(1)} %copy-done.16), kind=kCustom, calls=%fused_computation.10 | custom fusion | bytes 14712832 | tf_op jit(solution)/shard_map/gather | solution.py:71
  951.2 10.2 convolution_bitcast_fusion
  971.0 38.2 %gather_fusion.11 = bf16[8192,448]{1,0:T(8,128)(2,1)} fusion(bf16[8192,448]{1,0:T(8,128)(2,1)} %bitcast.252, s32[8192]{0:T(1024)S(1)} %copy-done.17), kind=kCustom, calls=%fused_computation.11 | custom fusion | bytes 14712832 | tf_op jit(solution)/shard_map/gather | solution.py:71
  1028.2 11.1 copy.151
  1039.3 38.4 %gather_fusion.7 = bf16[8192,448]{1,0:T(8,128)(2,1)} fusion(bf16[8192,448]{1,0:T(8,128)(2,1)} %copy.151, s32[8192]{0:T(1024)S(1)} %copy-done.16), kind=kCustom, calls=%fused_computation.7 | custom fusion | bytes 14712832 | tf_op jit(solution)/shard_map/gather | solution.py:71
  1077.7 10.2 convolution_bitcast_fusion.2
  1097.5 38.2 %gather_fusion.9 = bf16[8192,448]{1,0:T(8,128)(2,1)} fusion(bf16[8192,448]{1,0:T(8,128)(2,1)} %bitcast.249, s32[8192]{0:T(1024)S(1)} %copy-done.17), kind=kCustom, calls=%fused_computation.9 | custom fusion | bytes 14712832 | tf_op jit(solution)/shard_map/gather | solution.py:71
  1160.4 79.7 %custom-call.26 = f32[2,2,4,1,64,64]{4,5,3,2,1,0:T(8,128)S(1)} custom-call(f32[2,2,4,1,64,64]{5,4,3,2,1,0:T(8,128)} %get-tuple-element.40), custom_call_target="InvertDiagBlocksLowerTriangular" | custom-call | tf_op jit(solution)/shard_map/transpose(jvp(jit(cholesky)))/triangular_solve/custom-call.0 | solution.py:18
  1240.2 199.5 %all-reduce.3.cloned.1.call-done = f32[2,2,128,64,64]{4,3,2,1,0:T(8,128)} async-done(((f32[2,2,128,64,64]{4,3,2,1,0:T(8,128)}), f32[2,2,128,64,64]{4,3,2,1,0:T(8,128)}) %all-reduce.3.cloned.1.call-update) | async-done | bytes 8388624
  (195 shorter events, 256.7 us)
Async XLA Ops:
  55.0 29.6 %copy-start.12 = (bf16[256,448]{0,1:T(8,128)(2,1)S(1)}, bf16[256,448]{0,1:T(8,128)(2,1)}, u32[]{:S(2)}) copy-start(bf16[256,448]{0,1:T(8,128)(2,1)} %copy.198) | copy-start | bytes 688132
  93.9 208.6 %all-to-all-start = ((bf16[32,256,448]{1,2,0:T(8,128)(2,1)}), bf16[32,256,448]{1,2,0:T(8,128)(2,1)}, u32[]{:S(2)}, u32[]{:S(2)}) async-start(bf16[32,256,448]{1,2,0:T(8,128)(2,1)} %bitcast_dynamic-update-slice_fusion), calls=%async_computation | async-start | bytes 14680064 | tf_op jit(solution)/shard_map/all_to_all | solution.py:111
  101.3 478.0 %all-gather.6.cloned.1.call-start = ((), (), s32[]{:S(2)}) async-start(), calls=%async_computation.3 | async-start | bytes 8650752 | tf_op jit(solution)/shard_map/all_gather | solution.py:108
  112.2 194.5 %copy-start.8 = (f32[2,2,4,64,64]{4,3,2,1,0:T(8,128)S(1)}, f32[2,2,4,64,64]{4,3,2,1,0:T(8,128)}, u32[]{:S(2)}) copy-start(f32[2,2,4,64,64]{4,3,2,1,0:T(8,128)} %param.13) | copy-start | bytes 786436
  302.5 334.8 %all-to-all-start.1 = ((bf16[256,32,448]{0,2,1:T(8,128)(2,1)}), bf16[256,32,448]{0,2,1:T(8,128)(2,1)}, u32[]{:S(2)}, u32[]{:S(2)}) async-start(bf16[256,32,448]{0,2,1:T(8,128)(2,1)} %bitcast.271), calls=%async_computation.1 | async-start | bytes 14680064 | tf_op jit(solution)/shard_map/all_to_all | solution.py:116
  306.2 180.3 %copy-start.24 = (s32[2,13]{1,0:T(2,128)S(1)}, s32[2,13]{1,0:T(2,128)}, u32[]{:S(2)}) copy-start(s32[2,13]{1,0:T(2,128)} %param.14) | copy-start | bytes 316
  306.2 380.3 %all-gather.4.cloned.1.call-start = ((), (), s32[]{:S(2)}) async-start(), calls=%async_computation.2 | async-start | bytes 8650752 | tf_op jit(solution)/shard_map/all_gather | solution.py:101
  307.0 179.5 %copy-start = (f32[2,2,4,64,64]{4,3,2,1,0:T(8,128)}, f32[2,2,4,64,64]{4,3,2,1,0:T(8,128)S(1)}, u32[]{:S(2)}) copy-start(f32[2,2,4,64,64]{4,3,2,1,0:T(8,128)S(1)} %bitcast_subtract_fusion.1) | copy-start | bytes 786436
  307.9 225.0 %copy-start.13 = (f32[64,64]{1,0:T(8,128)}, f32[64,64]{1,0:T(8,128)S(1)}, u32[]{:S(2)}) copy-start(f32[64,64]{1,0:T(8,128)S(1)} %get-tuple-element.53) | copy-start | bytes 49156
  482.3 50.6 %copy-start.2 = (f32[2,2,4,1,64,64]{4,5,3,2,1,0:T(8,128)}, f32[2,2,4,1,64,64]{4,5,3,2,1,0:T(8,128)S(1)}, u32[]{:S(2)}) copy-start(f32[2,2,4,1,64,64]{4,5,3,2,1,0:T(8,128)S(1)} %custom-call.22) | copy-start | bytes 786436
  486.4 953.3 %all-reduce.3.cloned.1.call-start = ((), (), s32[]{:S(2)}) async-start(), calls=%async_computation.4 | async-start | bytes 33554432
  487.2 45.7 %copy-start.15 = (s32[8192]{0:T(1024)}, s32[8192]{0:T(1024)S(1)}, u32[]{:S(2)}) copy-start(s32[8192]{0:T(1024)S(1)} %broadcast_clamp_fusion.3) | copy-start | bytes 98308
  878.0 17.7 %slice-start = ((s8[6291456]{0:T(1024)(128)(4,1)}), s8[4194304]{0:T(1024)(128)(4,1)S(1)}, s32[]{:S(2)}) async-start(s8[6291456]{0:T(1024)(128)(4,1)} %bitcast.272), calls=%async_computation.5 | async-start | bytes 8388608
  901.7 11.1 copy-start.16
  961.4 9.7 copy-start.17
  1160.3 279.4 %copy-start.3 = (f32[2,2,4,1,64,64]{4,5,3,2,1,0:T(8,128)S(1)}, f32[2,2,4,1,64,64]{4,5,3,2,1,0:T(8,128)}, u32[]{:S(2)}) copy-start(f32[2,2,4,1,64,64]{4,5,3,2,1,0:T(8,128)} %copy-done.2) | copy-start | bytes 786436
  1160.3 281.5 %copy-start.7 = (f32[2,2,4,64,64]{4,3,2,1,0:T(8,128)S(1)}, f32[2,2,4,64,64]{4,3,2,1,0:T(8,128)}, u32[]{:S(2)}) copy-start(f32[2,2,4,64,64]{4,3,2,1,0:T(8,128)} %copy-done.6) | copy-start | bytes 786436
  1160.3 283.1 %copy-start.9 = (f32[2,2,4,64,64]{4,3,2,1,0:T(8,128)S(1)}, f32[2,2,4,64,64]{4,3,2,1,0:T(8,128)}, u32[]{:S(2)}) copy-start(f32[2,2,4,64,64]{4,3,2,1,0:T(8,128)} %get-tuple-element.47) | copy-start | bytes 786436
  1160.3 285.2 %copy-start.19 = (pred[64,64]{1,0:T(8,128)(4,1)S(1)}, pred[64,64]{1,0:T(8,128)(4,1)}, u32[]{:S(2)}) copy-start(pred[64,64]{1,0:T(8,128)(4,1)} %copy-done.18) | copy-start | bytes 12292
  1160.3 286.8 %copy-start.11 = (f32[2,2,4,64,64]{4,3,2,1,0:T(8,128)S(1)}, f32[2,2,4,64,64]{4,3,2,1,0:T(8,128)}, u32[]{:S(2)}) copy-start(f32[2,2,4,64,64]{4,3,2,1,0:T(8,128)} %copy-done.10) | copy-start | bytes 786436
  1160.4 286.8 %copy-start.23 = (pred[2,2,4]{2,1,0:T(4,128)(4,1)S(1)}, pred[2,2,4]{2,1,0:T(4,128)(4,1)}, u32[]{:S(2)}) copy-start(pred[2,2,4]{2,1,0:T(4,128)(4,1)} %copy-done.22) | copy-start | bytes 52
  1240.2 210.0 %copy-start.1 = (f32[2,2,4,64,64]{4,3,2,1,0:T(8,128)S(1)}, f32[2,2,4,64,64]{4,3,2,1,0:T(8,128)}, u32[]{:S(2)}) copy-start(f32[2,2,4,64,64]{4,3,2,1,0:T(8,128)} %copy-done) | copy-start | bytes 786436
  1240.2 210.0 %copy-start.20 = (pred[64,64]{1,0:T(8,128)(4,1)S(1)}, pred[64,64]{1,0:T(8,128)(4,1)}, u32[]{:S(2)}) copy-start(pred[64,64]{1,0:T(8,128)(4,1)} %get-tuple-element.44) | copy-start | bytes 12292
  1240.2 210.0 %copy-start.21 = (pred[64,64]{1,0:T(8,128)(4,1)S(1)}, pred[64,64]{1,0:T(8,128)(4,1)}, u32[]{:S(2)}) copy-start(pred[64,64]{1,0:T(8,128)(4,1)} %get-tuple-element.45) | copy-start | bytes 12292
  (9 other events, 44.9 us)
Sparse Core Ops, SparseCore 0:
  105.0 163.7 all-gather.5
  486.5 78.5 all-gather.3
  1160.5 279.2 all-reduce.2
